TPU v7x, 128 devices: a whole 4x4x4 slice. The times are simulated.
128 devices in a mesh: row: 8 (over z, x_lo), col: 16 (over y, x_hi, core).
Axes of the slice: x: 4 (x_hi: 2, x_lo: 2; x = x_hi * 2 + x_lo), y: 4, z: 4, core: 2. Of those that a mesh axis runs over, the one named last changes fastest.
Arguments:
- tensor_blocks: bfloat16 [8, 384, 6, 128, 128], P('row', 'col'), may hold values from -6 to 6
- block_list: int32 [8, 384, 2], P('row', 'col'), may hold values from 0 to 15, as said below
- occ_green: bfloat16 [2048, 2048], P(('row', 'col')), may hold values from -0.125 to 0.125
- virt_green: bfloat16 [2048, 2048], P(None, ('row', 'col')), may hold values from -0.125 to 0.125
Outputs:
- polarizability: float32 [8, 6, 6], P('row')
Inputs may be any that keep to these rules, and one draw needn't show every extreme that they name: `block_list`: within the 24 blocks of one device the (m, l) pairs are distinct, every atom block occurs as l once or twice and as m once or twice, so at most 2 blocks of one device share an l, and some l is shared by exactly 2.
All inputs are finite; a program needn't handle non-finite values.
Results may differ from a plain program's by a relative error of at most 0.006.
Values may be sent and summed in bfloat16 or wider, within the bound.
No kernel may reach another device: no remote copies, remote signals or barrier semaphores. Data moves between devices by JAX's collectives and lax.ppermute only.
A program may use at most 128 MiB of HBM per device.

v0:
```python
import jax
import jax.numpy as jnp
from jax import lax
from jax.sharding import PartitionSpec as P

CAP = 2


def shards(tensor_blocks, block_list, occ_green, virt_green):
    col_count = lax.axis_size("col")
    blocks = tensor_blocks[0]
    pairs = block_list[0]
    held = blocks.shape[0]
    width = blocks.shape[-1]
    target = pairs[:, 1]
    first_blocks = pairs[:, 0]
    places = jnp.arange(held)
    slot_rank = jnp.sum(
        (target[None, :] == target[:, None]) & (places[None, :] < places[:, None]), axis=1
    )
    select = (target[:, None, None] == jnp.arange(col_count)[None, :, None]) & (
        slot_rank[:, None, None] == jnp.arange(CAP)[None, None, :]
    )
    send_blocks = jnp.einsum(
        "tdk,tpab->dkpab", select.astype(jnp.bfloat16), blocks, preferred_element_type=jnp.float32
    ).astype(jnp.bfloat16)
    send_first = jnp.sum(select.astype(jnp.int32) * (first_blocks + 1)[:, None, None], axis=0) - 1
    recv_blocks, recv_first = (
        lax.all_to_all(send_blocks, "col", split_axis=0, concat_axis=0, tiled=True),
        lax.all_to_all(send_first, "col", split_axis=0, concat_axis=0, tiled=True),
    )
    slot_total = recv_blocks.shape[0] * recv_blocks.shape[1]
    flat_blocks = recv_blocks.reshape(slot_total, recv_blocks.shape[2], width, width)
    placing = (recv_first.reshape(slot_total)[:, None] == jnp.arange(col_count)[None, :]).astype(
        jnp.bfloat16
    )
    dense_parts = jnp.einsum(
        "sm,spab->pmab", placing, flat_blocks, preferred_element_type=jnp.float32
    )
    dense_tensor = dense_parts.astype(jnp.bfloat16).reshape(
        flat_blocks.shape[1], col_count * width, width
    )
    basis_total = dense_tensor.shape[1]
    occ_half = jnp.einsum(
        "nm,pml->pnl",
        lax.all_gather(occ_green, ("row", "col"), axis=0, tiled=True),
        dense_tensor,
        preferred_element_type=jnp.float32,
    ).astype(jnp.bfloat16)
    turned = lax.all_to_all(occ_half, "col", split_axis=1, concat_axis=2, tiled=True)
    both_sides = jnp.einsum(
        "pnl,ls->pns",
        turned,
        lax.all_gather(virt_green, ("row", "col"), axis=1, tiled=True),
        preferred_element_type=jnp.float32,
    ).astype(jnp.bfloat16)
    partial_polar = jnp.einsum(
        "pns,qsn->pq", both_sides, dense_tensor, preferred_element_type=jnp.float32
    )
    polar_total = lax.psum(partial_polar, "col")
    return (polar_total / float(basis_total))[None]


def solution(mesh):
    in_specs = (
        P("row", "col", None, None, None),
        P("row", "col", None),
        P(("row", "col"), None),
        P(None, ("row", "col")),
    )
    out_specs = P("row", None, None)
    return jax.shard_map(shards, mesh=mesh, in_specs=in_specs, out_specs=out_specs, check_vma=False)
```

profile of v0, /device:TPU:0, one launch (start us, length us, event | category | flops | bytes accessed | tf_op | source)
XLA Modules:
  0.0 585.8 jit_solution(11802510145233425043)
XLA Ops:
  6.5 0.7 all-gather.3.cloned.1.call-update
  7.3 0.7 all-gather.5.cloned.1.call-update
  8.0 0.8 add_bitcast_fusion.1
  9.1 0.7 copy.44
  9.8 7.1 %all-to-all-start.1 = ((s32[16,1,2]{2,1,0:T(1,128)}), s32[16,1,2]{2,1,0:T(1,128)S(1)}, u32[]{:S(2)}, u32[]{:S(2)}) async-start(s32[16,1,2]{2,1,0:T(1,128)} %copy.44), calls=%async_computation.1 | async-start | bytes 16384 | tf_op jit(solution)/shard_map/all_to_all | solution.py:30
  16.9 6.1 %fusion.11 = bf16[16,2,6,128,128]{4,0,3,2,1:T(8,128)(2,1)S(1)} fusion(bf16[24,6,128,128]{3,2,1,0:T(8,128)(2,1)} %bitcast.54, pred[24,2]{0,1:T(4,128)(4,1)S(1)} %iota_compare_fusion.3, pred[24,16]{0,1:T(8,128)(4,1)S(1)} %iota_compare_fusion.2), kind=kOutput, calls=%fused_computation.11 | convolution fusion | flops 154141440 | bytes 11010480 | tf_op jit(solution)/shard_map/tdk,tpab->dkpab/dot_general | solution.py:24
  23.0 4.3 copy.43
  27.4 7.3 %all-to-all-start = ((bf16[16,2,6,128,128]{4,3,2,1,0:T(8,128)(2,1)}), bf16[16,2,6,128,128]{4,3,2,1,0:T(8,128)(2,1)}, u32[]{:S(2)}, u32[]{:S(2)}) async-start(bf16[16,2,6,128,128]{4,3,2,1,0:T(8,128)(2,1)} %copy.43), calls=%async_computation | async-start | bytes 12582912 | tf_op jit(solution)/shard_map/all_to_all | solution.py:29
  35.2 0.7 reduce.3
  35.9 78.0 %all-to-all-done = bf16[16,2,6,128,128]{4,3,2,1,0:T(8,128)(2,1)} async-done(((bf16[16,2,6,128,128]{4,3,2,1,0:T(8,128)(2,1)}), bf16[16,2,6,128,128]{4,3,2,1,0:T(8,128)(2,1)}, u32[]{:S(2)}, u32[]{:S(2)}) %all-to-all-start) | async-done | bytes 6291488 | tf_op jit(solution)/shard_map/all_to_all | solution.py:29
  113.9 6.6 %convert_bitcast_fusion = bf16[6,16,128,128]{3,1,2,0:T(8,128)(2,1)S(1)} fusion(bf16[32,6,128,128]{3,2,1,0:T(8,128)(2,1)} %bitcast.6, s32[32]{0:T(128)S(1)} %eq.73), kind=kOutput, calls=%fused_computation.14 | convolution fusion | flops 102236672 | bytes 9437312 | tf_op jit(solution)/shard_map/sm,spab->pmab/dot_general | solution.py:37
  120.5 0.8 copy.46
  121.3 159.5 %all-gather.3.cloned.1.call-done = bf16[2048,2048]{1,0:T(8,128)(2,1)} async-done(((bf16[16,2048]{1,0:T(8,128)(2,1)}), bf16[2048,2048]{1,0:T(8,128)(2,1)}) %all-gather.3.cloned.1.call-update) | async-done | bytes 8388624 | tf_op jit(solution)/shard_map/all_gather | solution.py:46
  280.8 10.3 %fusion.20 = bf16[6,2048,128]{1,2,0:T(8,128)(2,1)} fusion(bf16[6,2048,128]{2,1,0:T(8,128)(2,1)S(1)} %bitcast.52, bf16[2048,2048]{1,0:T(8,128)(2,1)} %all-gather.3.cloned.1.call-done), kind=kOutput, calls=%fused_computation.15 | convolution fusion | flops 6444023808 | bytes 14680064 | tf_op jit(solution)/shard_map/nm,pml->pnl/dot_general | solution.py:44
  291.2 6.4 %copy.48 = bf16[6,2048,128]{2,0,1:T(8,128)(2,1)} copy(bf16[6,2048,128]{1,2,0:T(8,128)(2,1)} %fusion.20) | data formatting | bytes 6291456 | tf_op jit(solution)/shard_map/convert_element_type | solution.py:49
  297.6 5.4 all-to-all-start.2
  303.0 5.1 copy.53
  308.0 51.2 %all-to-all-done.2 = bf16[6,2048,128]{2,0,1:T(8,128)(2,1)} async-done(((bf16[6,2048,128]{2,0,1:T(8,128)(2,1)}), bf16[6,2048,128]{2,0,1:T(8,128)(2,1)}, u32[]{:S(2)}, u32[]{:S(2)}) %all-to-all-start.2) | async-done | bytes 3145760 | tf_op jit(solution)/shard_map/all_to_all | solution.py:50
  359.3 5.4 copy.50
  364.7 164.0 %all-gather.5.cloned.1.call-done = bf16[2048,2048]{0,1:T(8,128)(2,1)} async-done(((bf16[2048,16]{0,1:T(8,128)(2,1)}), bf16[2048,2048]{0,1:T(8,128)(2,1)}) %all-gather.5.cloned.1.call-update) | async-done | bytes 8388624 | tf_op jit(solution)/shard_map/all_gather | solution.py:54
  528.7 9.3 %fusion.17 = bf16[6,128,2048]{2,1,0:T(8,128)(2,1)S(1)} fusion(bf16[6,128,2048]{1,2,0:T(8,128)(2,1)S(1)} %bitcast.55, bf16[2048,2048]{0,1:T(8,128)(2,1)} %all-gather.5.cloned.1.call-done), kind=kOutput, calls=%fused_computation.13 | convolution fusion | flops 6444023808 | bytes 14680064 | tf_op jit(solution)/shard_map/pnl,ls->pns/dot_general | solution.py:51
  538.0 5.7 fusion.25
  543.7 34.6 %psum.7 = f32[6,6]{1,0:T(8,128)S(1)} all-reduce(f32[6,6]{1,0:T(8,128)S(1)} %fusion.25), channel_id=1, replica_groups=mesh['row'=8,'col'=16] {'col'}, use_global_device_ids=true, to_apply=%region_2.0 | all-reduce | flops 36 | bytes 288 | tf_op jit(solution)/shard_map/psum | solution.py:60
  578.4 0.6 copy.54
  (13 shorter events, 1.0 us)
Async XLA Ops:
  6.5 274.3 %all-gather.3.cloned.1.call-start = ((), (), s32[]{:S(2)}) async-start(), calls=%async_computation.3 | async-start | bytes 8454144 | tf_op jit(solution)/shard_map/all_gather | solution.py:46
  7.3 521.5 %all-gather.5.cloned.1.call-start = ((), (), s32[]{:S(2)}) async-start(), calls=%async_computation.4 | async-start | bytes 8454144 | tf_op jit(solution)/shard_map/all_gather | solution.py:54
  9.8 17.6 %all-to-all-start.1 = ((s32[16,1,2]{2,1,0:T(1,128)}), s32[16,1,2]{2,1,0:T(1,128)S(1)}, u32[]{:S(2)}, u32[]{:S(2)}) async-start(s32[16,1,2]{2,1,0:T(1,128)} %copy.44), calls=%async_computation.1 | async-start | bytes 16384 | tf_op jit(solution)/shard_map/all_to_all | solution.py:30
  27.4 86.5 %all-to-all-start = ((bf16[16,2,6,128,128]{4,3,2,1,0:T(8,128)(2,1)}), bf16[16,2,6,128,128]{4,3,2,1,0:T(8,128)(2,1)}, u32[]{:S(2)}, u32[]{:S(2)}) async-start(bf16[16,2,6,128,128]{4,3,2,1,0:T(8,128)(2,1)} %copy.43), calls=%async_computation | async-start | bytes 12582912 | tf_op jit(solution)/shard_map/all_to_all | solution.py:29
  297.6 61.7 %all-to-all-start.2 = ((bf16[6,2048,128]{2,0,1:T(8,128)(2,1)}), bf16[6,2048,128]{2,0,1:T(8,128)(2,1)}, u32[]{:S(2)}, u32[]{:S(2)}) async-start(bf16[6,2048,128]{2,0,1:T(8,128)(2,1)} %copy.48), calls=%async_computation.2 | async-start | bytes 8388608 | tf_op jit(solution)/shard_map/all_to_all | solution.py:50
  528.7 9.3 %copy-start = (bf16[6,2048,128]{1,0,2:T(8,128)(2,1)S(1)}, bf16[6,2048,128]{1,0,2:T(8,128)(2,1)}, u32[]{:S(2)}) copy-start(bf16[6,2048,128]{1,0,2:T(8,128)(2,1)} %copy.53) | copy-start | bytes 9437188
Sparse Core Ops, SparseCore 0:
  9.1 271.7 all-gather.2
  282.6 246.1 all-gather.4
where the time goes:
time: 586 us
  waiting for transfers between devices  454 us (77%)
  matrix products  38 us (6%)
  blocking collectives  34.6 us (6%)
  local copies, waits for them, and re-layouts  23.9 us (4%)
  starting transfers between devices  19.8 us (3%)
  between operations  13.5 us (2%)
    all_gather x1, waiting for transfers between devices, shards(): lax.all_gather(virt_green, ('row', 'col'), axis=1, tiled=True)  164 us
    all_gather x1, waiting for transfers between devices, shards(): lax.all_gather(occ_green, ('row', 'col'), axis=0, tiled=True)  160 us
    all_to_all x1, waiting for transfers between devices, shards(): lax.all_to_all(send_blocks, 'col', split_axis=0, concat_axis=0, tiled=True)  78 us
    all_to_all x1, waiting for transfers between devices, shards(): lax.all_to_all(occ_half, 'col', split_axis=1, concat_axis=2, tiled=True)  51.2 us
    psum x1, blocking collectives, shards(): polar_total = lax.psum(partial_polar, 'col')  34.6 us
  transfers between devices with their start and end apart: 5, of which 4 were waited for; matrix products, arithmetic and copies ran while one was open for 8% of the time, Pallas kernels for 0%

commit v1 on v0

--- a/solution.py
+++ b/solution.py
@@ -2,6 +2,7 @@
 import jax.numpy as jnp
 from jax import lax
 from jax.sharding import PartitionSpec as P
+from jax.lax import all_to_all, axis_size
 
 CAP = 2
 
@@ -48,11 +49,11 @@
         preferred_element_type=jnp.float32,
     ).astype(jnp.bfloat16)
     turned = lax.all_to_all(occ_half, "col", split_axis=1, concat_axis=2, tiled=True)
+    obtain_wall = lambda xs: jnp.concatenate(
+        all_to_all(jnp.stack(axis_size(("row", "col")) * [xs]), ("row", "col"), 0, 0), axis=1
+    )
     both_sides = jnp.einsum(
-        "pnl,ls->pns",
-        turned,
-        lax.all_gather(virt_green, ("row", "col"), axis=1, tiled=True),
-        preferred_element_type=jnp.float32,
+        "pnl,ls->pns", turned, obtain_wall(virt_green), preferred_element_type=jnp.float32
     ).astype(jnp.bfloat16)
     partial_polar = jnp.einsum(
         "pns,qsn->pq", both_sides, dense_tensor, preferred_element_type=jnp.float32

time: 586 us -> 522 us (0.89)
  waiting for transfers between devices: 454 us -> 328 us
  blocking collectives: 34.6 us -> 90.6 us
    all_gather x1 -> x0, waiting for transfers between devices: 164 us -> none  [shards(): lax.all_gather(virt_green, ('row', 'col'), axis=1, tiled=True)]
    all_to_all x0 -> x1, blocking collectives: none -> 56.9 us  [shards(): lax.all_to_all(occ_half, 'col', split_axis=1, concat_axis=2, tiled=True)]
    all_to_all x1, waiting for transfers between devices: 51.2 us -> 89.9 us  [shards(): all_to_all(jnp.stack(axis_size(('row', 'col')) * [xs]), ('row', 'col'), 0...]
  transfers between devices with their start and end apart: 5 -> 4, of which waited for: 4 -> 3; matrix products, arithmetic and copies ran while one was open for 8% -> 6% of each run, Pallas kernels for 0% -> 0%
where the time goes in v1:
time: 522 us; the launch traced here: 521 us
  waiting for transfers between devices  328 us (63%)
  blocking collectives  90.6 us (17%)
  matrix products  38 us (7%)
  local copies, waits for them, and re-layouts  28.1 us (5%)
  starting transfers between devices  20.5 us (4%)
  between operations  13.5 us (3%)
    all_gather x1, waiting for transfers between devices, shards(): lax.all_gather(occ_green, ('row', 'col'), axis=0, tiled=True)  160 us
    all_to_all x1, waiting for transfers between devices, shards(): all_to_all(jnp.stack(axis_size(('row', 'col')) * [xs]), ('row', 'col'), 0...  89.9 us
    all_to_all x1, waiting for transfers between devices, shards(): lax.all_to_all(send_blocks, 'col', split_axis=0, concat_axis=0, tiled=True)  77.7 us
    all_to_all x1, blocking collectives, shards(): lax.all_to_all(occ_half, 'col', split_axis=1, concat_axis=2, tiled=True)  56.9 us
    psum x1, blocking collectives, shards(): polar_total = lax.psum(partial_polar, 'col')  33.7 us
  transfers between devices with their start and end apart: 4, of which 3 were waited for; matrix products, arithmetic and copies ran while one was open for 6% of the time, Pallas kernels for 0%

profile of v1, /device:TPU:0, one launch (start us, length us, event | category | flops | bytes accessed | tf_op | source)
XLA Modules:
  0.0 520.9 jit_solution(3034065534698460837)
XLA Ops:
  6.5 0.7 all-gather.2.cloned.1.call-update
  7.3 0.8 add_bitcast_fusion.1
  8.3 0.7 copy.47
  9.0 7.1 %all-to-all-start.1 = ((s32[16,1,2]{2,1,0:T(1,128)}), s32[16,1,2]{2,1,0:T(1,128)S(1)}, u32[]{:S(2)}, u32[]{:S(2)}) async-start(s32[16,1,2]{2,1,0:T(1,128)} %copy.47), calls=%async_computation.1 | async-start | bytes 16384 | tf_op jit(solution)/shard_map/all_to_all | solution.py:31
  16.2 6.1 %fusion.9 = bf16[16,2,6,128,128]{4,0,3,2,1:T(8,128)(2,1)S(1)} fusion(bf16[24,6,128,128]{3,2,1,0:T(8,128)(2,1)} %bitcast.56, pred[24,2]{0,1:T(4,128)(4,1)S(1)} %iota_compare_fusion.3, pred[24,16]{0,1:T(8,128)(4,1)S(1)} %iota_compare_fusion.2), kind=kOutput, calls=%fused_computation.9 | convolution fusion | flops 154141440 | bytes 11010480 | tf_op jit(solution)/shard_map/tdk,tpab->dkpab/dot_general | solution.py:25
  22.3 4.4 copy.46
  26.7 7.3 %all-to-all-start = ((bf16[16,2,6,128,128]{4,3,2,1,0:T(8,128)(2,1)}), bf16[16,2,6,128,128]{4,3,2,1,0:T(8,128)(2,1)}, u32[]{:S(2)}, u32[]{:S(2)}) async-start(bf16[16,2,6,128,128]{4,3,2,1,0:T(8,128)(2,1)} %copy.46), calls=%async_computation | async-start | bytes 12582912 | tf_op jit(solution)/shard_map/all_to_all | solution.py:30
  34.5 0.7 reduce.3
  35.2 77.7 %all-to-all-done = bf16[16,2,6,128,128]{4,3,2,1,0:T(8,128)(2,1)} async-done(((bf16[16,2,6,128,128]{4,3,2,1,0:T(8,128)(2,1)}), bf16[16,2,6,128,128]{4,3,2,1,0:T(8,128)(2,1)}, u32[]{:S(2)}, u32[]{:S(2)}) %all-to-all-start) | async-done | bytes 6291488 | tf_op jit(solution)/shard_map/all_to_all | solution.py:30
  112.9 6.6 %convert_bitcast_fusion = bf16[6,16,128,128]{3,1,2,0:T(8,128)(2,1)S(1)} fusion(bf16[32,6,128,128]{3,2,1,0:T(8,128)(2,1)} %bitcast.6, s32[32]{0:T(128)S(1)} %eq.73), kind=kOutput, calls=%fused_computation.12 | convolution fusion | flops 102236672 | bytes 9437312 | tf_op jit(solution)/shard_map/sm,spab->pmab/dot_general | solution.py:38
  119.5 0.8 copy.49
  120.3 160.0 %all-gather.2.cloned.1.call-done = bf16[2048,2048]{1,0:T(8,128)(2,1)} async-done(((bf16[16,2048]{1,0:T(8,128)(2,1)}), bf16[2048,2048]{1,0:T(8,128)(2,1)}) %all-gather.2.cloned.1.call-update) | async-done | bytes 8388624 | tf_op jit(solution)/shard_map/all_gather | solution.py:47
  280.4 10.3 %fusion.15 = bf16[6,2048,128]{1,2,0:T(8,128)(2,1)} fusion(bf16[6,2048,128]{2,1,0:T(8,128)(2,1)S(1)} %bitcast.54, bf16[2048,2048]{1,0:T(8,128)(2,1)} %all-gather.2.cloned.1.call-done), kind=kOutput, calls=%fused_computation.13 | convolution fusion | flops 6444023808 | bytes 14680064 | tf_op jit(solution)/shard_map/nm,pml->pnl/dot_general | solution.py:45
  290.7 6.3 %copy.51 = bf16[6,2048,128]{2,0,1:T(8,128)(2,1)} copy(bf16[6,2048,128]{1,2,0:T(8,128)(2,1)} %fusion.15) | data formatting | bytes 6291456 | tf_op jit(solution)/shard_map/convert_element_type | solution.py:50
  297.0 56.9 %all_to_all.34 = bf16[6,2048,128]{2,0,1:T(8,128)(2,1)} all-to-all(bf16[6,2048,128]{2,0,1:T(8,128)(2,1)} %copy.51), channel_id=1, replica_groups=mesh['row'=8,'col'=16] {'col'}, dimensions={1} | all-to-all | bytes 6291456 | tf_op jit(solution)/shard_map/all_to_all | solution.py:51
  353.9 4.3 stack.2
  358.2 6.1 %all-to-all-start.3 = ((bf16[128,2048,16]{1,2,0:T(8,128)(2,1)}), bf16[128,2048,16]{1,2,0:T(8,128)(2,1)}, u32[]{:S(2)}, u32[]{:S(2)}) async-start(bf16[128,2048,16]{1,2,0:T(8,128)(2,1)} %stack.2), calls=%async_computation.3 | async-start | bytes 16777216 | tf_op jit(solution)/shard_map/all_to_all | solution.py:53
  364.3 5.0 copy.57
  369.3 5.4 %copy.53 = bf16[6,128,16,128]{1,3,2,0:T(8,128)(2,1)S(1)} copy(bf16[6,128,16,128]{3,0,1,2:T(8,128)(2,1)} %bitcast.53) | data formatting | bytes 6291456 | tf_op jit(solution)/shard_map/all_to_all | solution.py:51
  374.8 89.9 %all-to-all-done.3 = bf16[128,2048,16]{1,2,0:T(8,128)(2,1)} async-done(((bf16[128,2048,16]{1,2,0:T(8,128)(2,1)}), bf16[128,2048,16]{1,2,0:T(8,128)(2,1)}, u32[]{:S(2)}, u32[]{:S(2)}) %all-to-all-start.3) | async-done | bytes 8388640 | tf_op jit(solution)/shard_map/all_to_all | solution.py:53
  464.7 9.3 %convolution_convert_fusion = bf16[6,128,2048]{2,1,0:T(8,128)(2,1)S(1)} fusion(bf16[6,128,2048]{1,2,0:T(8,128)(2,1)S(1)} %bitcast.57, bf16[2048,2048,1]{0,1,2:T(8,128)(2,1)} %bitcast.21), kind=kOutput, calls=%fused_computation.11 | convolution fusion | flops 6444023808 | bytes 14680064 | tf_op jit(solution)/shard_map/pnl,ls->pns/dot_general | solution.py:55
  474.0 5.7 %fusion.20 = f32[6,6]{1,0:T(8,128)S(1)} fusion(bf16[6,2048,128]{1,0,2:T(8,128)(2,1)S(1)} %copy-done, bf16[6,128,2048]{2,1,0:T(8,128)(2,1)S(1)} %convolution_convert_fusion), kind=kOutput, calls=%fused_computation.14 | convolution fusion | flops 18874368 | bytes 6291600 | tf_op jit(solution)/shard_map/pns,qsn->pq/dot_general | solution.py:58
  479.7 33.7 %psum.7 = f32[6,6]{1,0:T(8,128)S(1)} all-reduce(f32[6,6]{1,0:T(8,128)S(1)} %fusion.20), channel_id=1, replica_groups=mesh['row'=8,'col'=16] {'col'}, use_global_device_ids=true, to_apply=%region_2.0 | all-reduce | flops 36 | bytes 288 | tf_op jit(solution)/shard_map/psum | solution.py:61
  513.4 0.6 copy.58
  (14 shorter events, 0.9 us)
Async XLA Ops:
  6.5 273.8 %all-gather.2.cloned.1.call-start = ((), (), s32[]{:S(2)}) async-start(), calls=%async_computation.4 | async-start | bytes 8454144 | tf_op jit(solution)/shard_map/all_gather | solution.py:47
  9.0 17.6 %all-to-all-start.1 = ((s32[16,1,2]{2,1,0:T(1,128)}), s32[16,1,2]{2,1,0:T(1,128)S(1)}, u32[]{:S(2)}, u32[]{:S(2)}) async-start(s32[16,1,2]{2,1,0:T(1,128)} %copy.47), calls=%async_computation.1 | async-start | bytes 16384 | tf_op jit(solution)/shard_map/all_to_all | solution.py:31
  26.7 86.2 %all-to-all-start = ((bf16[16,2,6,128,128]{4,3,2,1,0:T(8,128)(2,1)}), bf16[16,2,6,128,128]{4,3,2,1,0:T(8,128)(2,1)}, u32[]{:S(2)}, u32[]{:S(2)}) async-start(bf16[16,2,6,128,128]{4,3,2,1,0:T(8,128)(2,1)} %copy.46), calls=%async_computation | async-start | bytes 12582912 | tf_op jit(solution)/shard_map/all_to_all | solution.py:30
  297.0 56.9 %copy-start.1 = (bf16[2048,16]{0,1:T(8,128)(2,1)S(1)}, bf16[2048,16]{0,1:T(8,128)(2,1)}, u32[]{:S(2)}) copy-start(bf16[2048,16]{0,1:T(8,128)(2,1)} %param.7) | copy-start | bytes 196612
  358.2 106.5 %all-to-all-start.3 = ((bf16[128,2048,16]{1,2,0:T(8,128)(2,1)}), bf16[128,2048,16]{1,2,0:T(8,128)(2,1)}, u32[]{:S(2)}, u32[]{:S(2)}) async-start(bf16[128,2048,16]{1,2,0:T(8,128)(2,1)} %stack.2), calls=%async_computation.3 | async-start | bytes 16777216 | tf_op jit(solution)/shard_map/all_to_all | solution.py:53
  464.7 9.3 %copy-start = (bf16[6,2048,128]{1,0,2:T(8,128)(2,1)S(1)}, bf16[6,2048,128]{1,0,2:T(8,128)(2,1)}, u32[]{:S(2)}) copy-start(bf16[6,2048,128]{1,0,2:T(8,128)(2,1)} %copy.57) | copy-start | bytes 9437188
Sparse Core Ops, SparseCore 0:
  9.1 271.2 all-gather.1
